TPU v7x, 128 devices: a whole 4x4x4 slice. The times are simulated.
128 devices in a mesh: row: 8 (over y, z_hi), col: 16 (over x, z_lo, core).
Axes of the slice: x: 4, y: 4, z: 4 (z_hi: 2, z_lo: 2; z = z_hi * 2 + z_lo), core: 2. Of those that a mesh axis runs over, the one named last changes fastest.
Arguments:
- adjacency: bfloat16 [32768, 32768], P('row', 'col'), as said below
- tile_mask: int32 [256, 256], P('row', 'col'), may hold values from 0 to 1, as said below
- out_grad: bfloat16 [32768, 256], P(('row', 'col')), may hold values from -6 to 6
- pre_two: bfloat16 [32768, 256], P(('row', 'col')), may hold values from -6 to 6
- hidden: bfloat16 [32768, 256], P(('col', 'row')), may hold values from -24 to 24
- pre_one: bfloat16 [32768, 256], P(('col', 'row')), may hold values from -6 to 6
- features: bfloat16 [32768, 256], P(('row', 'col')), may hold values from -6 to 6
- w_two: bfloat16 [256, 256], replicated, may hold values from -0.375 to 0.375
- w_one: bfloat16 [256, 256], replicated, may hold values from -0.375 to 0.375
Outputs:
- node_grad: bfloat16 [32768, 256], P(('row', 'col'))
- weight_grad_one: float32 [256, 256], replicated
- weight_grad_two: float32 [256, 256], replicated
Inputs may be any that keep to these rules, and one draw needn't show every extreme that they name: adjacency is symmetric and nonnegative. tile_mask is symmetric and every diagonal tile is 1.
All inputs are finite; a program needn't handle non-finite values.
Results may differ from a plain program's by a relative error of at most 0.02.
Values may be sent and summed in bfloat16 or wider, within the bound.
A program may use at most 128 MiB of HBM per device.

v0:
```python
import jax
import jax.numpy as jnp
from jax import lax
from jax.sharding import PartitionSpec as P


def tile_pick(count, tile_size, tile_total):
    node_ids = lax.broadcasted_iota(jnp.int32, (count, 1), 0)
    tile_ids = lax.broadcasted_iota(jnp.int32, (1, tile_total), 1)
    return (node_ids // tile_size == tile_ids).astype(jnp.bfloat16)


def local(adjacency, tile_mask, out_grad, pre_two, hidden, pre_one, features, w_two, w_one):
    tile_rows, tile_cols = tile_mask.shape
    tile_size = adjacency.shape[0] // tile_rows
    mask_values = tile_mask.astype(jnp.bfloat16)
    shard_nodes = out_grad.shape[0]
    weight_scale = 4.0 * shard_nodes ** (-0.5)
    contract_rows = (((0,), (0,)), ((), ()))
    contract_cols = (((1,), (1,)), ((), ()))
    grad_two = jnp.where(pre_two > 0, out_grad, jnp.zeros_like(out_grad))
    shard_rows = lax.all_gather(grad_two, "col", axis=0, tiled=True)
    count = shard_rows.shape[0]
    strip_rows = adjacency
    picker = tile_pick(count, tile_size, tile_rows)
    strip_mask = jnp.dot(picker, mask_values, preferred_element_type=jnp.float32).astype(
        jnp.bfloat16
    )
    strip_rows = (strip_rows.reshape(count, tile_cols, tile_size) * strip_mask[:, :, None]).reshape(
        count, adjacency.shape[1]
    )
    column_part = lax.dot_general(
        strip_rows, shard_rows, contract_rows, preferred_element_type=jnp.float32
    )
    column_part = column_part.astype(jnp.bfloat16).astype(jnp.float32)
    prop_two = lax.psum_scatter(
        column_part.astype(jnp.bfloat16), "row", scatter_dimension=0, tiled=True
    )
    back_grad = lax.dot_general(prop_two, w_two, contract_cols, preferred_element_type=jnp.float32)
    grad_one = jnp.where(pre_one > 0, back_grad, jnp.zeros_like(back_grad)).astype(jnp.bfloat16)
    shard_rows = lax.all_gather(grad_one, "row", axis=0, tiled=True)
    count = shard_rows.shape[0]
    strip_cols = adjacency
    picker = tile_pick(count, tile_size, tile_cols)
    strip_mask = lax.dot_general(
        mask_values, picker, contract_cols, preferred_element_type=jnp.float32
    ).astype(jnp.bfloat16)
    strip_cols = (strip_cols.reshape(tile_rows, tile_size, count) * strip_mask[:, None, :]).reshape(
        adjacency.shape[0], count
    )
    row_part = jnp.dot(strip_cols, shard_rows, preferred_element_type=jnp.float32)
    term_two = lax.dot_general(hidden, prop_two, contract_rows, preferred_element_type=jnp.float32)
    summed_two = lax.psum(term_two, ("row", "col"))
    row_part = row_part.astype(jnp.bfloat16).astype(jnp.float32)
    prop_one = lax.psum_scatter(
        row_part.astype(jnp.bfloat16), "col", scatter_dimension=0, tiled=True
    )
    term_one = lax.dot_general(
        features, prop_one, contract_rows, preferred_element_type=jnp.float32
    )
    node_grad = lax.dot_general(
        prop_one, w_one, contract_cols, preferred_element_type=jnp.float32
    ).astype(jnp.bfloat16)
    summed_one = lax.psum(term_one, ("row", "col"))
    return (node_grad, summed_one * weight_scale, summed_two * weight_scale)


def solution(mesh):
    return jax.shard_map(
        local,
        mesh=mesh,
        in_specs=(
            P("row", "col"),
            P("row", "col"),
            P(("row", "col"), None),
            P(("row", "col"), None),
            P(("col", "row"), None),
            P(("col", "row"), None),
            P(("row", "col"), None),
            P(),
            P(),
        ),
        out_specs=(P(("row", "col"), None), P(), P()),
        check_vma=False,
    )
```

profile of v0, /device:TPU:1, one launch (start us, length us, event | category | flops | bytes accessed | tf_op | source)
XLA Modules:
  0.0 437.8 jit_solution(10373811274106707431)
XLA Ops:
  7.2 0.0 copy-start
  7.2 0.0 all-gather.3.cloned.1.call-start
  7.2 1.7 compare_select_fusion
  8.9 0.0 all-gather.3.cloned.1.call-update
  8.9 0.0 reduce-scatter.3.cloned.1.call-start
  9.0 0.9 convolution_convert_fusion.1
  9.9 0.5 copy.15
  10.4 37.4 %all-gather.3.cloned.1.call-done = bf16[4096,256]{1,0:T(8,128)(2,1)} async-done(((bf16[256,256]{1,0:T(8,128)(2,1)}), bf16[4096,256]{1,0:T(8,128)(2,1)}) %all-gather.3.cloned.1.call-update) | async-done | bytes 2097168 | tf_op jit(solution)/shard_map/all_gather | solution.py:22
  47.7 0.0 copy-start.7
  47.7 18.8 %mul.31 = bf16[4096,16,128]{2,1,0:T(8,128)(2,1)} broadcast(bf16[4096,16]{1,0:T(8,128)(2,1)S(1)} %copy.15), dimensions={0,1} | broadcast | bytes 16908288 | tf_op jit(solution)/shard_map/mul | solution.py:29
  66.5 0.0 copy-done.7
  66.5 0.0 copy-start.3
  66.5 0.0 copy-start.6
  66.5 14.3 %fusion.2 = bf16[2048,256]{1,0:T(8,128)(2,1)} fusion(bf16[4096,256]{1,0:T(8,128)(2,1)S(1)} %copy-done.7, bf16[4096,2048]{1,0:T(8,128)(2,1)} %param.9, bf16[512,8,16,128]{3,2,1,0:T(8,128)(2,1)} %bitcast.25), kind=kOutput, calls=%fused_computation.6 | convolution fusion | flops 4303880192 | bytes 36700160 | tf_op jit(solution)/shard_map/dot_general | solution.py:32
  80.9 0.0 reduce-scatter.3.cloned.1.call-update
  80.9 0.0 all-gather.5.cloned.1.call-start
  80.9 70.7 %reduce-scatter.3.cloned.1.call-done = bf16[256,256]{1,0:T(8,128)(2,1)} async-done(((bf16[2048,256]{1,0:T(8,128)(2,1)}), bf16[256,256]{1,0:T(8,128)(2,1)}) %reduce-scatter.3.cloned.1.call-update) | async-done | bytes 131088 | tf_op jit(solution)/shard_map/reduce_scatter | solution.py:36
  151.6 0.0 copy-done
  151.6 0.0 copy-done.3
  151.6 1.8 fusion.4
  153.4 0.0 all-gather.5.cloned.1.call-update
  153.4 0.0 reduce-scatter.5.cloned.1.call-start
  153.5 0.0 copy-done.6
  153.5 0.5 fusion.3
  154.0 13.9 %bitcast_multiply_fusion.2 = bf16[4096,2048]{1,0:T(8,128)(2,1)} fusion(bf16[4096,2048]{1,0:T(8,128)(2,1)} %param.9, bf16[32,2048]{1,0:T(8,128)(2,1)S(1)} %fusion.3), kind=kLoop, calls=%fused_computation.3 | loop fusion | flops 8388608 | bytes 33685504 | tf_op jit(solution)/shard_map/mul | solution.py:48
  167.9 0.0 copy-start.1
  167.9 0.0 copy-start.4
  167.9 0.0 copy-start.5
  167.9 0.0 copy-start.2
  167.9 33.0 %all-gather.5.cloned.1.call-done = bf16[2048,256]{1,0:T(8,128)(2,1)} async-done(((bf16[256,256]{1,0:T(8,128)(2,1)}), bf16[2048,256]{1,0:T(8,128)(2,1)}) %all-gather.5.cloned.1.call-update) | async-done | bytes 1048592 | tf_op jit(solution)/shard_map/all_gather | solution.py:41
  201.0 11.9 %convolution_convert_fusion = bf16[4096,256]{1,0:T(8,128)(2,1)} fusion(bf16[4096,2048]{1,0:T(8,128)(2,1)} %bitcast_multiply_fusion.2, bf16[2048,256]{1,0:T(8,128)(2,1)} %all-gather.5.cloned.1.call-done), kind=kOutput, calls=%fused_computation.4 | convolution fusion | flops 4296015872 | bytes 19922944 | tf_op jit(solution)/shard_map/dot_general | solution.py:51
  212.9 0.0 reduce-scatter.5.cloned.1.call-update
  212.9 0.0 all-reduce.3.cloned.1.call-start
  212.9 0.0 copy-done.1
  212.9 0.0 copy-done.4
  213.0 0.9 convolution_bitcast_fusion
  213.9 60.4 %reduce-scatter.5.cloned.1.call-done = bf16[256,256]{1,0:T(8,128)(2,1)} async-done(((bf16[4096,256]{1,0:T(8,128)(2,1)}), bf16[256,256]{1,0:T(8,128)(2,1)}) %reduce-scatter.5.cloned.1.call-update) | async-done | bytes 131088 | tf_op jit(solution)/shard_map/reduce_scatter | solution.py:55
  274.3 0.0 copy-done.5
  274.3 1.8 convolution_bitcast_fusion.1
  276.2 0.0 all-reduce.3.cloned.1.call-update
  276.2 0.0 copy-done.2
  276.2 1.8 convolution_convert_fusion.3
  278.0 150.5 %all-reduce.3.cloned.1.call-done = (f32[256,256]{0,1:T(8,128)}, f32[256,256]{0,1:T(8,128)}) async-done(((f32[256,256]{0,1:T(8,128)}, f32[256,256]{0,1:T(8,128)}), (f32[256,256]{0,1:T(8,128)}, f32[256,256]{0,1:T(8,128)})) %all-reduce.3.cloned.1.call-update) | async-done | bytes 524304 | tf_op jit(solution)/shard_map/psum | solution.py:64
  428.5 1.1 broadcast_multiply_fusion
  429.6 0.8 copy.16
  430.4 0.8 copy.17
  (2 shorter events, 0.0 us)
Async XLA Ops:
  7.2 144.5 %copy-start = (bf16[256,256]{1,0:T(8,128)(2,1)S(1)}, bf16[256,256]{1,0:T(8,128)(2,1)}, u32[]{:S(2)}) copy-start(bf16[256,256]{1,0:T(8,128)(2,1)} %param.16) | copy-start | bytes 393220
  7.2 40.5 %all-gather.3.cloned.1.call-start = ((), (), s32[]{:S(2)}) async-start(), calls=%async_computation.2 | async-start | bytes 2228224 | tf_op jit(solution)/shard_map/all_gather | solution.py:22
  8.9 142.7 %reduce-scatter.3.cloned.1.call-start = ((), (), s32[]{:S(2)}) async-start(), calls=%async_computation.3 | async-start | bytes 1179648 | tf_op jit(solution)/shard_map/reduce_scatter | solution.py:36
  47.7 18.8 %copy-start.7 = (bf16[4096,256]{1,0:T(8,128)(2,1)S(1)}, bf16[4096,256]{1,0:T(8,128)(2,1)}, u32[]{:S(2)}) copy-start(bf16[4096,256]{1,0:T(8,128)(2,1)} %all-gather.3.cloned.1.call-done) | copy-start | bytes 6291460
  66.5 85.1 %copy-start.3 = (bf16[256,256]{1,0:T(8,128)(2,1)S(1)}, bf16[256,256]{1,0:T(8,128)(2,1)}, u32[]{:S(2)}) copy-start(bf16[256,256]{1,0:T(8,128)(2,1)} %param.14) | copy-start | bytes 393220
  66.5 87.0 %copy-start.6 = (s32[32,16]{0,1:T(8,128)S(1)}, s32[32,16]{0,1:T(8,128)}, u32[]{:S(2)}) copy-start(s32[32,16]{0,1:T(8,128)} %param.10) | copy-start | bytes 6148
  80.9 120.1 %all-gather.5.cloned.1.call-start = ((), (), s32[]{:S(2)}) async-start(), calls=%async_computation.4 | async-start | bytes 1179648 | tf_op jit(solution)/shard_map/all_gather | solution.py:41
  153.4 120.9 %reduce-scatter.5.cloned.1.call-start = ((), (), s32[]{:S(2)}) async-start(), calls=%async_computation.5 | async-start | bytes 2228224 | tf_op jit(solution)/shard_map/reduce_scatter | solution.py:55
  167.9 45.0 %copy-start.1 = (bf16[256,256]{1,0:T(8,128)(2,1)S(1)}, bf16[256,256]{1,0:T(8,128)(2,1)}, u32[]{:S(2)}) copy-start(bf16[256,256]{1,0:T(8,128)(2,1)} %reduce-scatter.3.cloned.1.call-done) | copy-start | bytes 393220
  167.9 45.0 %copy-start.4 = (bf16[256,256]{1,0:T(8,128)(2,1)S(1)}, bf16[256,256]{1,0:T(8,128)(2,1)}, u32[]{:S(2)}) copy-start(bf16[256,256]{1,0:T(8,128)(2,1)} %param.13) | copy-start | bytes 393220
  167.9 106.4 %copy-start.5 = (bf16[256,256]{1,0:T(8,128)(2,1)S(1)}, bf16[256,256]{1,0:T(8,128)(2,1)}, u32[]{:S(2)}) copy-start(bf16[256,256]{1,0:T(8,128)(2,1)} %param.15) | copy-start | bytes 393220
  167.9 108.2 %copy-start.2 = (bf16[256,256]{1,0:T(8,128)(2,1)S(1)}, bf16[256,256]{1,0:T(8,128)(2,1)}, u32[]{:S(2)}) copy-start(bf16[256,256]{1,0:T(8,128)(2,1)} %param.17) | copy-start | bytes 393220
  212.9 215.6 %all-reduce.3.cloned.1.call-start = ((), (), s32[]{:S(2)}) async-start(), calls=%async_computation.6 | async-start | bytes 1048576 | tf_op jit(solution)/shard_map/psum | solution.py:64
Sparse Core Ops, SparseCore 0:
  10.3 37.4 all-gather.2
  81.0 70.5 reduce-scatter.2
  154.5 46.3 all-gather.4
  213.0 61.2 reduce-scatter.4
  279.7 148.7 all-reduce.2
where the time goes:
time: 438 us
  waiting for transfers between devices  352 us (80%)
  matrix products  33.9 us (8%)
  local copies, waits for them, and re-layouts  21 us (5%)
  other arithmetic  16.7 us (4%)
  between operations  13.9 us (3%)
    psum x1, waiting for transfers between devices, local(): summed_one = lax.psum(term_one, ('row', 'col'))  151 us
    reduce_scatter x1, waiting for transfers between devices, local(): lax.psum_scatter(column_part.astype(jnp.bfloat16), 'row', scatter_dimensi...  70.7 us
    reduce_scatter x1, waiting for transfers between devices, local(): lax.psum_scatter(row_part.astype(jnp.bfloat16), 'col', scatter_dimension=...  60.4 us
    all_gather x1, waiting for transfers between devices, local(): shard_rows = lax.all_gather(grad_two, 'col', axis=0, tiled=True)  37.4 us
    all_gather x1, waiting for transfers between devices, local(): shard_rows = lax.all_gather(grad_one, 'row', axis=0, tiled=True)  33 us
    mul x1, local copies, waits for them, and re-layouts, local(): strip_rows.reshape(count, tile_cols, tile_size) * strip_mask[:, :, None]  18.8 us
    dot_general x1, matrix products, local(): lax.dot_general(strip_rows, shard_rows, contract_rows, preferred_element_...  14.3 us
    mul x1, other arithmetic, local(): strip_cols.reshape(tile_rows, tile_size, count) * strip_mask[:, None, :]  13.9 us
  transfers between devices with their start and end apart: 5, of which 5 were waited for; matrix products, arithmetic and copies ran while one was open for 4% of the time, Pallas kernels for 0%

commit v1 on v0

--- a/solution.py
+++ b/solution.py
@@ -61,7 +61,7 @@
     node_grad = lax.dot_general(
         prop_one, w_one, contract_cols, preferred_element_type=jnp.float32
     ).astype(jnp.bfloat16)
-    summed_one = lax.psum(term_one, ("row", "col"))
+    summed_one = jnp.sum(lax.all_gather(term_one, ("row", "col")), axis=0)
     return (node_grad, summed_one * weight_scale, summed_two * weight_scale)
 
 

time: 438 us -> 690 us (1.58)
  waiting for transfers between devices: 352 us -> 579 us
  local copies, waits for them, and re-layouts: 21 us -> 40.6 us
    all_gather x0 -> x1, waiting for transfers between devices: none -> 230 us  [local(): summed_one = jnp.sum(lax.all_gather(term_one, ('row', 'col')), axis=0)]
    unnamed x18 -> x21, local copies, waits for them, and re-layouts: 1.71 us -> 21.3 us
  transfers between devices with their start and end apart: 5 -> 6, of which waited for: 5 -> 6; matrix products, arithmetic and copies ran while one was open for 4% -> 3% of each run, Pallas kernels for 0% -> 0%
where the time goes in v1:
time: 690 us; the launch traced here: 689 us
  waiting for transfers between devices  579 us (84%)
  local copies, waits for them, and re-layouts  40.6 us (6%)
  matrix products  33.9 us (5%)
  other arithmetic  20.7 us (3%)
  between operations  14.2 us (2%)
    all_gather x1, waiting for transfers between devices, local(): summed_one = jnp.sum(lax.all_gather(term_one, ('row', 'col')), axis=0)  230 us
    psum x1, waiting for transfers between devices, local(): summed_two = lax.psum(term_two, ('row', 'col'))  148 us
    reduce_scatter x1, waiting for transfers between devices, local(): lax.psum_scatter(column_part.astype(jnp.bfloat16), 'row', scatter_dimensi...  70.7 us
    reduce_scatter x1, waiting for transfers between devices, local(): lax.psum_scatter(row_part.astype(jnp.bfloat16), 'col', scatter_dimension=...  60.3 us
    all_gather x1, waiting for transfers between devices, local(): shard_rows = lax.all_gather(grad_two, 'col', axis=0, tiled=True)  37.4 us
    all_gather x1, waiting for transfers between devices, local(): shard_rows = lax.all_gather(grad_one, 'row', axis=0, tiled=True)  33.1 us
    unnamed x21, local copies, waits for them, and re-layouts  21.3 us
    mul x1, local copies, waits for them, and re-layouts, local(): strip_rows.reshape(count, tile_cols, tile_size) * strip_mask[:, :, None]  18.8 us
  transfers between devices with their start and end apart: 6, of which 6 were waited for; matrix products, arithmetic and copies ran while one was open for 3% of the time, Pallas kernels for 0%

profile of v1, /device:TPU:1, one launch (start us, length us, event | category | flops | bytes accessed | tf_op | source)
XLA Modules:
  0.0 689.2 jit_solution(14412068116893561795)
XLA Ops:
  7.2 0.0 copy-start
  7.2 0.0 all-gather.5.cloned.1.call-start
  7.2 1.7 compare_select_fusion
  8.9 0.0 all-gather.5.cloned.1.call-update
  8.9 0.0 reduce-scatter.3.cloned.1.call-start
  9.0 0.9 convolution_convert_fusion.1
  9.9 0.5 copy.15
  10.4 37.4 %all-gather.5.cloned.1.call-done = bf16[4096,256]{1,0:T(8,128)(2,1)} async-done(((bf16[256,256]{1,0:T(8,128)(2,1)}), bf16[4096,256]{1,0:T(8,128)(2,1)}) %all-gather.5.cloned.1.call-update) | async-done | bytes 2097168 | tf_op jit(solution)/shard_map/all_gather | solution.py:22
  47.7 0.0 copy-start.8
  47.7 18.8 %mul.31 = bf16[4096,16,128]{2,1,0:T(8,128)(2,1)} broadcast(bf16[4096,16]{1,0:T(8,128)(2,1)S(1)} %copy.15), dimensions={0,1} | broadcast | bytes 16908288 | tf_op jit(solution)/shard_map/mul | solution.py:29
  66.5 0.0 copy-done.8
  66.5 0.0 copy-start.4
  66.5 0.0 copy-start.7
  66.5 14.3 %fusion.2 = bf16[2048,256]{1,0:T(8,128)(2,1)} fusion(bf16[4096,256]{1,0:T(8,128)(2,1)S(1)} %copy-done.8, bf16[4096,2048]{1,0:T(8,128)(2,1)} %param.9, bf16[512,8,16,128]{3,2,1,0:T(8,128)(2,1)} %bitcast.31), kind=kOutput, calls=%fused_computation.7 | convolution fusion | flops 4303880192 | bytes 36700160 | tf_op jit(solution)/shard_map/dot_general | solution.py:32
  80.8 0.0 reduce-scatter.3.cloned.1.call-update
  80.9 0.0 all-gather.7.cloned.1.call-start
  80.9 70.7 %reduce-scatter.3.cloned.1.call-done = bf16[256,256]{1,0:T(8,128)(2,1)} async-done(((bf16[2048,256]{1,0:T(8,128)(2,1)}), bf16[256,256]{1,0:T(8,128)(2,1)}) %reduce-scatter.3.cloned.1.call-update) | async-done | bytes 131088 | tf_op jit(solution)/shard_map/reduce_scatter | solution.py:36
  151.6 0.0 copy-done
  151.6 0.0 copy-done.4
  151.6 1.8 fusion.4
  153.4 0.0 all-gather.7.cloned.1.call-update
  153.4 0.0 reduce-scatter.5.cloned.1.call-start
  153.5 0.0 copy-done.7
  153.5 0.5 fusion.3
  154.0 13.9 %bitcast_multiply_fusion.2 = bf16[4096,2048]{1,0:T(8,128)(2,1)} fusion(bf16[4096,2048]{1,0:T(8,128)(2,1)} %param.9, bf16[32,2048]{1,0:T(8,128)(2,1)S(1)} %fusion.3), kind=kLoop, calls=%fused_computation.4 | loop fusion | flops 8388608 | bytes 33685504 | tf_op jit(solution)/shard_map/mul | solution.py:48
  167.9 33.1 %all-gather.7.cloned.1.call-done = bf16[2048,256]{1,0:T(8,128)(2,1)} async-done(((bf16[256,256]{1,0:T(8,128)(2,1)}), bf16[2048,256]{1,0:T(8,128)(2,1)}) %all-gather.7.cloned.1.call-update) | async-done | bytes 1048592 | tf_op jit(solution)/shard_map/all_gather | solution.py:41
  201.0 11.9 %convolution_convert_fusion = bf16[4096,256]{1,0:T(8,128)(2,1)} fusion(bf16[4096,2048]{1,0:T(8,128)(2,1)} %bitcast_multiply_fusion.2, bf16[2048,256]{1,0:T(8,128)(2,1)} %all-gather.7.cloned.1.call-done), kind=kOutput, calls=%fused_computation.5 | convolution fusion | flops 4296015872 | bytes 19922944 | tf_op jit(solution)/shard_map/dot_general | solution.py:51
  212.8 0.0 reduce-scatter.5.cloned.1.call-update
  212.9 0.0 all-reduce.2.cloned.1.call-start
  212.9 0.0 copy-done.2
  212.9 0.0 copy-done.5
  212.9 0.9 convolution_bitcast_fusion
  213.9 0.0 all-reduce.2.cloned.1.call-update
  213.9 0.2 all-gather.9.cloned.1.call-start
  214.1 60.3 %reduce-scatter.5.cloned.1.call-done = bf16[256,256]{1,0:T(8,128)(2,1)} async-done(((bf16[4096,256]{1,0:T(8,128)(2,1)}), bf16[256,256]{1,0:T(8,128)(2,1)}) %reduce-scatter.5.cloned.1.call-update) | async-done | bytes 131088 | tf_op jit(solution)/shard_map/reduce_scatter | solution.py:55
  274.4 0.0 copy-done.6
  274.4 1.8 convolution_bitcast_fusion.1
  276.3 0.0 all-gather.9.cloned.1.call-update
  276.3 148.3 %all-reduce.2.cloned.1.call-done = f32[256,256]{0,1:T(8,128)} async-done(((f32[256,256]{0,1:T(8,128)}), f32[256,256]{0,1:T(8,128)}) %all-reduce.2.cloned.1.call-update) | async-done | bytes 262160 | tf_op jit(solution)/shard_map/psum | solution.py:53
  424.6 1.0 broadcast_multiply_fusion
  425.5 0.8 copy.17
  426.4 0.0 copy-done.3
  426.4 1.8 convolution_convert_fusion.3
  428.1 229.6 %all-gather.9.cloned.1.call-done = f32[32768,256]{0,1:T(8,128)} async-done(((f32[256,256]{0,1:T(8,128)}), f32[32768,256]{0,1:T(8,128)}) %all-gather.9.cloned.1.call-update) | async-done | bytes 33554448 | tf_op jit(solution)/shard_map/all_gather | solution.py:64
  657.7 19.6 %copy.19 = f32[32,8,128,256]{3,2,1,0:T(8,128)S(1)} copy(f32[32,8,128,256]{3,1,2,0:T(8,128)} %bitcast.30) | data formatting | bytes 67108864
  677.4 4.1 bitcast_reduce_fusion
  681.5 0.8 copy.16
  682.4 0.0 copy-done.1
  (8 shorter events, 0.0 us)
Async XLA Ops:
  7.2 144.4 %copy-start = (bf16[256,256]{1,0:T(8,128)(2,1)S(1)}, bf16[256,256]{1,0:T(8,128)(2,1)}, u32[]{:S(2)}) copy-start(bf16[256,256]{1,0:T(8,128)(2,1)} %param.16) | copy-start | bytes 393220
  7.2 40.5 %all-gather.5.cloned.1.call-start = ((), (), s32[]{:S(2)}) async-start(), calls=%async_computation.2 | async-start | bytes 2228224 | tf_op jit(solution)/shard_map/all_gather | solution.py:22
  8.9 142.7 %reduce-scatter.3.cloned.1.call-start = ((), (), s32[]{:S(2)}) async-start(), calls=%async_computation.3 | async-start | bytes 1179648 | tf_op jit(solution)/shard_map/reduce_scatter | solution.py:36
  47.7 18.8 %copy-start.8 = (bf16[4096,256]{1,0:T(8,128)(2,1)S(1)}, bf16[4096,256]{1,0:T(8,128)(2,1)}, u32[]{:S(2)}) copy-start(bf16[4096,256]{1,0:T(8,128)(2,1)} %all-gather.5.cloned.1.call-done) | copy-start | bytes 6291460
  66.5 85.1 %copy-start.4 = (bf16[256,256]{1,0:T(8,128)(2,1)S(1)}, bf16[256,256]{1,0:T(8,128)(2,1)}, u32[]{:S(2)}) copy-start(bf16[256,256]{1,0:T(8,128)(2,1)} %param.14) | copy-start | bytes 393220
  66.5 87.0 %copy-start.7 = (s32[32,16]{0,1:T(8,128)S(1)}, s32[32,16]{0,1:T(8,128)}, u32[]{:S(2)}) copy-start(s32[32,16]{0,1:T(8,128)} %param.10) | copy-start | bytes 6148
  80.9 120.1 %all-gather.7.cloned.1.call-start = ((), (), s32[]{:S(2)}) async-start(), calls=%async_computation.4 | async-start | bytes 1179648 | tf_op jit(solution)/shard_map/all_gather | solution.py:41
  153.4 121.0 %reduce-scatter.5.cloned.1.call-start = ((), (), s32[]{:S(2)}) async-start(), calls=%async_computation.5 | async-start | bytes 2228224 | tf_op jit(solution)/shard_map/reduce_scatter | solution.py:55
  167.9 45.0 %copy-start.2 = (bf16[256,256]{1,0:T(8,128)(2,1)S(1)}, bf16[256,256]{1,0:T(8,128)(2,1)}, u32[]{:S(2)}) copy-start(bf16[256,256]{1,0:T(8,128)(2,1)} %reduce-scatter.3.cloned.1.call-done) | copy-start | bytes 393220
  167.9 45.0 %copy-start.5 = (bf16[256,256]{1,0:T(8,128)(2,1)S(1)}, bf16[256,256]{1,0:T(8,128)(2,1)}, u32[]{:S(2)}) copy-start(bf16[256,256]{1,0:T(8,128)(2,1)} %param.13) | copy-start | bytes 393220
  167.9 106.5 %copy-start.6 = (bf16[256,256]{1,0:T(8,128)(2,1)S(1)}, bf16[256,256]{1,0:T(8,128)(2,1)}, u32[]{:S(2)}) copy-start(bf16[256,256]{1,0:T(8,128)(2,1)} %param.15) | copy-start | bytes 393220
  167.9 258.5 %copy-start.3 = (bf16[256,256]{1,0:T(8,128)(2,1)S(1)}, bf16[256,256]{1,0:T(8,128)(2,1)}, u32[]{:S(2)}) copy-start(bf16[256,256]{1,0:T(8,128)(2,1)} %param.17) | copy-start | bytes 393220
  212.9 211.7 %all-reduce.2.cloned.1.call-start = ((), (), s32[]{:S(2)}) async-start(), calls=%async_computation.6 | async-start | bytes 524288 | tf_op jit(solution)/shard_map/psum | solution.py:53
  213.9 443.9 %all-gather.9.cloned.1.call-start = ((), (), s32[]{:S(2)}) async-start(), calls=%async_computation.7 | async-start | bytes 33816576 | tf_op jit(solution)/shard_map/all_gather | solution.py:64
  657.7 24.6 %copy-start.1 = (bf16[256,256]{1,0:T(8,128)(2,1)S(1)}, bf16[256,256]{1,0:T(8,128)(2,1)}, u32[]{:S(2)}) copy-start(bf16[256,256]{1,0:T(8,128)(2,1)} %param.16) | copy-start | bytes 393220
Sparse Core Ops, SparseCore 0:
  10.3 37.4 all-gather.4
  81.0 70.5 reduce-scatter.2
  154.5 46.3 all-gather.6
  213.0 61.4 reduce-scatter.4
  279.6 144.9 all-reduce.1
  426.7 230.9 all-gather.8
